TPU v7x, 256 devices: a whole 4x4x8 slice. The times are simulated.
256 devices in a mesh: dp: 2 (over z_hi), context: 8 (over y, core), tensor: 16 (over z_lo, x).
Axes of the slice: x: 4, y: 4, z: 8 (z_hi: 2, z_lo: 4; z = z_hi * 4 + z_lo), core: 2. Of those that a mesh axis runs over, the one named last changes fastest.
Arguments:
- tokens: bfloat16 [2, 4096, 5376], P('dp', ('context', 'tensor')), may hold values from -48 to 48
- output_gradient: bfloat16 [2, 4096, 5376], P('dp', ('context', 'tensor')), may hold values from -48 to 48
- document_index: int32 [2, 4096], P('dp'), may hold values from 0 to 3, never falling along the last dimension, each value on 1 to 2048 neighbouring positions
- query_weight: bfloat16 [5376, 4096], P(None, 'tensor'), may hold values from -1 to 1
- key_value_weight: bfloat16 [2, 5376, 2048], P(None, None, 'tensor'), may hold values from -1 to 1
- output_weight: bfloat16 [4096, 5376], P('tensor'), may hold values from -0.09375 to 0.09375
- adapter_down_projections: bfloat16 [3, 16, 5376], replicated, may hold values from -0.078125 to 0.078125
- adapter_up_query: bfloat16 [16, 4096], P(None, 'tensor'), may hold values from -0.29882812 to 0.29882812
- adapter_up_key_value: bfloat16 [2, 16, 2048], P(None, None, 'tensor'), may hold values from -0.29882812 to 0.29882812
- adapter_down_output: bfloat16 [16, 4096], P(None, 'tensor'), may hold values from -0.09375 to 0.09375
- adapter_up_output: bfloat16 [16, 5376], replicated, may hold values from -0.29882812 to 0.29882812
Outputs:
- grad_input: bfloat16 [2, 4096, 5376], P('dp', ('context', 'tensor'))
- grad_down_qkv: float32 [3, 16, 5376], replicated
- query_up_gradient: float32 [16, 4096], P(None, 'tensor')
- grad_up_keyvalue: float32 [2, 16, 2048], P(None, None, 'tensor')
- grad_down_out: float32 [16, 4096], P(None, 'tensor')
- output_up_gradient: float32 [16, 5376], replicated
Inputs may be any that keep to these rules, and one draw needn't show every extreme that they name: `document_index`: ids never fall along a sequence; each document holds 1 to half of 4096 tokens, and one holds exactly that many.
All inputs are finite; a program needn't handle non-finite values.
Results may differ from a plain program's by a relative error of at most 0.03.
Values may be sent and summed in bfloat16 or wider, within the bound.
No kernel may reach another device: no remote copies, remote signals or barrier semaphores. Data moves between devices by JAX's collectives and lax.ppermute only.
A program may use at most 128 MiB of HBM per device.

v0:
```python
import jax
import jax.numpy as jnp
from jax import lax
from jax.sharding import PartitionSpec as P

HEAD_SIZE = 128
WINDOW = 1024
adapter_scale = 2.0
attn_scale = 168.0 ** (-0.5)
rope_base = 10000.0


def passed_along(block, axis, distance):
    devices = range(lax.axis_size(axis))
    route = [(i - distance, i) for i in devices if i - distance in devices]
    return lax.ppermute(block, axis, route)


def rope_tables(positions, head_width):
    half_width = head_width // 2
    inverse = rope_base ** (-(jnp.arange(half_width, dtype=jnp.float32) * 2.0 / head_width))
    angle = positions[:, None] * inverse[None, :]
    return (jnp.cos(angle), jnp.sin(angle))


def apply_rotation(vectors, cosine_table, sine_values):
    half_width = vectors.shape[-1] // 2
    front_half = vectors[..., :half_width]
    back_half = vectors[..., half_width:]
    cosine_table = cosine_table[:, None, :]
    sine_values = sine_values[:, None, :]
    return jnp.concatenate(
        [
            front_half * cosine_table - back_half * sine_values,
            back_half * cosine_table + front_half * sine_values,
        ],
        -1,
    )


def undo_rotation(grads, cosine_table, sine_values):
    half_width = grads.shape[-1] // 2
    front_half = grads[..., :half_width]
    back_half = grads[..., half_width:]
    cosine_table = cosine_table[:, None, :]
    sine_values = sine_values[:, None, :]
    return jnp.concatenate(
        [
            front_half * cosine_table + back_half * sine_values,
            back_half * cosine_table - front_half * sine_values,
        ],
        -1,
    )


def band_block(queries, key_rows, value_rows, attention_output_gradient, allowed):
    row_count, heads_q, head_width = queries.shape
    heads_kv = key_rows.shape[1]
    group_size = heads_q // heads_kv
    query_groups = queries.reshape(row_count, heads_kv, group_size, head_width)
    grad_groups = attention_output_gradient.reshape(row_count, heads_kv, group_size, head_width)
    scores = (
        jnp.einsum("chgd,khd->hgck", query_groups, key_rows, preferred_element_type=jnp.float32)
        * attn_scale
    )
    scores = jnp.where(allowed[None, None], scores, -1e30)
    row_max = jnp.max(scores, -1, keepdims=True)
    exponent = jnp.exp(scores - row_max)
    weights = exponent / jnp.sum(exponent, -1, keepdims=True)
    weights_low = weights.astype(jnp.bfloat16)
    attention_output = jnp.einsum(
        "hgck,khd->chgd", weights_low, value_rows, preferred_element_type=jnp.float32
    ).astype(jnp.bfloat16)
    grad_weights = jnp.einsum(
        "chgd,khd->hgck", grad_groups, value_rows, preferred_element_type=jnp.float32
    )
    row_dot = jnp.einsum(
        "chgd,chgd->hgc", grad_groups.astype(jnp.float32), attention_output.astype(jnp.float32)
    )
    grad_scores = (weights * (grad_weights - row_dot[..., None]) * attn_scale).astype(jnp.bfloat16)
    query_gradient = jnp.einsum(
        "hgck,khd->chgd", grad_scores, key_rows, preferred_element_type=jnp.float32
    )
    key_gradient = jnp.einsum(
        "hgck,chgd->khd", grad_scores, query_groups, preferred_element_type=jnp.float32
    )
    value_gradient = jnp.einsum(
        "hgck,chgd->khd", weights_low, grad_groups, preferred_element_type=jnp.float32
    )
    return (
        attention_output.reshape(row_count, heads_q, head_width),
        query_gradient.reshape(row_count, heads_q, head_width),
        key_gradient,
        value_gradient,
    )


def local(
    tokens,
    output_gradient,
    document_index,
    query_weight,
    key_value_weight,
    output_weight,
    adapter_down_projections,
    adapter_up_query,
    adapter_up_key_value,
    adapter_down_output,
    adapter_up_output,
):
    tensor_size = lax.axis_size("tensor")
    context_at = lax.axis_index("context")
    local_count = tokens.shape[1]
    model_width_size = tokens.shape[2]
    shard_len = local_count * tensor_size
    halo_count = (WINDOW - 1) // shard_len + 1
    rank_width_size = adapter_down_projections.shape[1]
    heads_q = query_weight.shape[1] // HEAD_SIZE
    heads_kv = key_value_weight.shape[2] // HEAD_SIZE
    gathered, incoming_gradient = (
        lax.all_gather(tokens[0], "tensor", axis=0, tiled=True),
        lax.all_gather(output_gradient[0], "tensor", axis=0, tiled=True),
    )
    down_factors_all = adapter_down_projections.reshape(3 * rank_width_size, model_width_size)
    adapted = jnp.einsum(
        "ja,ma->jm", gathered, down_factors_all, preferred_element_type=jnp.float32
    ).astype(jnp.bfloat16)
    adapted_query = adapted[:, :rank_width_size]
    adapted_key = adapted[:, rank_width_size : 2 * rank_width_size]
    adapted_value = adapted[:, 2 * rank_width_size :]
    query_linear = jnp.dot(
        gathered, query_weight, preferred_element_type=jnp.float32
    ) + adapter_scale * jnp.dot(adapted_query, adapter_up_query, preferred_element_type=jnp.float32)
    key_linear = jnp.dot(
        gathered, key_value_weight[0], preferred_element_type=jnp.float32
    ) + adapter_scale * jnp.dot(
        adapted_key, adapter_up_key_value[0], preferred_element_type=jnp.float32
    )
    value_linear = jnp.dot(
        gathered, key_value_weight[1], preferred_element_type=jnp.float32
    ) + adapter_scale * jnp.dot(
        adapted_value, adapter_up_key_value[1], preferred_element_type=jnp.float32
    )
    positions = (context_at * shard_len + jnp.arange(shard_len, dtype=jnp.int32)).astype(
        jnp.float32
    )
    cosine_table, sine_values = rope_tables(positions, HEAD_SIZE)
    queries = apply_rotation(
        query_linear.reshape(shard_len, heads_q, HEAD_SIZE), cosine_table, sine_values
    ).astype(jnp.bfloat16)
    key_local = apply_rotation(
        key_linear.reshape(shard_len, heads_kv, HEAD_SIZE), cosine_table, sine_values
    ).astype(jnp.bfloat16)
    value_local = value_linear.reshape(shard_len, heads_kv, HEAD_SIZE).astype(jnp.bfloat16)
    pair_local = jnp.stack([key_local, value_local], 0)
    earlier = [
        passed_along(pair_local, "context", distance) for distance in range(halo_count, 0, -1)
    ]
    pairs = jnp.concatenate(earlier + [pair_local], 1)
    segment_row = document_index[0]
    segment_pad = jnp.concatenate(
        [jnp.full((halo_count * shard_len,), -1, jnp.int32), segment_row], 0
    )
    key_seg = lax.dynamic_slice_in_dim(
        segment_pad, context_at * shard_len, (halo_count + 1) * shard_len, 0
    )
    query_seg = lax.dynamic_slice_in_dim(segment_row, context_at * shard_len, shard_len, 0)
    query_pos = context_at * shard_len + jnp.arange(shard_len, dtype=jnp.int32)
    key_pos = (context_at - halo_count) * shard_len + jnp.arange(
        (halo_count + 1) * shard_len, dtype=jnp.int32
    )
    offset = query_pos[:, None] - key_pos[None, :]
    allowed = (
        (key_pos >= 0)[None, :]
        & (offset >= 0)
        & (offset < WINDOW)
        & (query_seg[:, None] == key_seg[None, :])
    )
    up_gradient = (
        adapter_scale
        * jnp.einsum(
            "ja,ma->jm", incoming_gradient, adapter_up_output, preferred_element_type=jnp.float32
        )
    ).astype(jnp.bfloat16)
    attention_output_gradient = (
        jnp.einsum(
            "td,hd->th", incoming_gradient, output_weight, preferred_element_type=jnp.float32
        )
        + jnp.dot(up_gradient, adapter_down_output, preferred_element_type=jnp.float32)
    ).astype(jnp.bfloat16)
    attention_output, grad_query_rot, grad_keys_all, grad_values_all = band_block(
        queries,
        pairs[0],
        pairs[1],
        attention_output_gradient.reshape(shard_len, heads_q, HEAD_SIZE),
        allowed,
    )
    grad_pairs = jnp.stack([grad_keys_all, grad_values_all], 0)

    def share_for(distance):
        return lax.slice_in_dim(
            grad_pairs,
            (halo_count - distance) * shard_len,
            (halo_count - distance + 1) * shard_len,
            axis=1,
        )

    combined = share_for(0)
    for distance in range(1, halo_count + 1):
        combined = combined + passed_along(
            share_for(distance).astype(jnp.bfloat16), "context", -distance
        ).astype(jnp.float32)
    attention_output_flat = attention_output.reshape(shard_len, heads_q * HEAD_SIZE)
    query_gradient = (
        undo_rotation(grad_query_rot, cosine_table, sine_values)
        .reshape(shard_len, heads_q * HEAD_SIZE)
        .astype(jnp.bfloat16)
    )
    key_gradient = (
        undo_rotation(combined[0], cosine_table, sine_values)
        .reshape(shard_len, heads_kv * HEAD_SIZE)
        .astype(jnp.bfloat16)
    )
    value_gradient = combined[1].reshape(shard_len, heads_kv * HEAD_SIZE).astype(jnp.bfloat16)
    query_hidden = (
        adapter_scale
        * jnp.einsum(
            "kn,pn->kp", query_gradient, adapter_up_query, preferred_element_type=jnp.float32
        )
    ).astype(jnp.bfloat16)
    key_hidden = (
        adapter_scale
        * jnp.einsum(
            "kn,pn->kp", key_gradient, adapter_up_key_value[0], preferred_element_type=jnp.float32
        )
    ).astype(jnp.bfloat16)
    value_hidden = (
        adapter_scale
        * jnp.einsum(
            "kn,pn->kp", value_gradient, adapter_up_key_value[1], preferred_element_type=jnp.float32
        )
    ).astype(jnp.bfloat16)
    hidden_all = jnp.concatenate([query_hidden, key_hidden, value_hidden], 1)
    grad_down_part = jnp.einsum(
        "tr,td->rd", hidden_all, gathered, preferred_element_type=jnp.float32
    ).reshape(3, rank_width_size, model_width_size)
    query_up_gradient_piece = adapter_scale * jnp.einsum(
        "tr,th->rh", adapted_query, query_gradient, preferred_element_type=jnp.float32
    )
    grad_up_kv_part = jnp.stack(
        [
            adapter_scale
            * jnp.einsum(
                "tr,th->rh", adapted_key, key_gradient, preferred_element_type=jnp.float32
            ),
            adapter_scale
            * jnp.einsum(
                "tr,th->rh", adapted_value, value_gradient, preferred_element_type=jnp.float32
            ),
        ],
        0,
    )
    grad_down_out_part = jnp.einsum(
        "tr,th->rh", up_gradient, attention_output_flat, preferred_element_type=jnp.float32
    )
    factor_part = jnp.einsum(
        "kn,pn->kp", attention_output_flat, adapter_down_output, preferred_element_type=jnp.float32
    )
    factor_value = lax.psum(factor_part.astype(jnp.bfloat16), "tensor")
    output_up_gradient_piece = adapter_scale * jnp.einsum(
        "tr,td->rd", factor_value, incoming_gradient, preferred_element_type=jnp.float32
    )
    grad_down_qkv = lax.psum(grad_down_part, ("dp", "context", "tensor"))
    query_up_gradient, grad_up_keyvalue, grad_down_out, output_up_gradient = (
        lax.psum(query_up_gradient_piece.astype(jnp.bfloat16), ("dp", "context")).astype(
            jnp.float32
        ),
        lax.psum(grad_up_kv_part.astype(jnp.bfloat16), ("dp", "context")).astype(jnp.float32),
        lax.psum(grad_down_out_part.astype(jnp.bfloat16), ("dp", "context")).astype(jnp.float32),
        lax.psum(output_up_gradient_piece.astype(jnp.bfloat16), ("dp", "context")).astype(
            jnp.float32
        ),
    )
    term = jnp.einsum("th,dh->td", query_gradient, query_weight, preferred_element_type=jnp.float32)
    term = term + jnp.einsum(
        "th,dh->td", key_gradient, key_value_weight[0], preferred_element_type=jnp.float32
    )
    term = term + jnp.einsum(
        "th,dh->td", value_gradient, key_value_weight[1], preferred_element_type=jnp.float32
    )
    full_sum = lax.psum(
        (term + jnp.dot(hidden_all, down_factors_all, preferred_element_type=jnp.float32)).astype(
            jnp.bfloat16
        ),
        "tensor",
    ).astype(jnp.float32)
    mine = lax.dynamic_slice_in_dim(
        full_sum, lax.axis_index("tensor") * local_count, local_count, 0
    )
    grad_input = mine.astype(jnp.bfloat16)[None]
    return (
        grad_input,
        grad_down_qkv,
        query_up_gradient,
        grad_up_keyvalue,
        grad_down_out,
        output_up_gradient,
    )


def solution(mesh):
    in_specs = (
        P("dp", ("context", "tensor"), None),
        P("dp", ("context", "tensor"), None),
        P("dp", None),
        P(None, "tensor"),
        P(None, None, "tensor"),
        P("tensor", None),
        P(),
        P(None, "tensor"),
        P(None, None, "tensor"),
        P(None, "tensor"),
        P(),
    )
    out_specs = (
        P("dp", ("context", "tensor"), None),
        P(),
        P(None, "tensor"),
        P(None, None, "tensor"),
        P(None, "tensor"),
        P(),
    )
    return jax.shard_map(local, mesh=mesh, in_specs=in_specs, out_specs=out_specs, check_vma=False)
```

profile of v0, /device:TPU:2, one launch (start us, length us, event | category | flops | bytes accessed | tf_op | source)
XLA Modules:
  0.0 926.9 jit_solution(11296037939888309069)
XLA Ops:
  7.2 0.7 all-gather.5.cloned.1.call-update
  8.0 0.7 all-gather.7.cloned.1.call-update
  8.8 0.7 constant_dynamic-slice_fusion
  9.5 0.8 pad_dynamic-slice_fusion
  10.3 1.8 multiply_cosine_fusion
  12.1 1.7 fusion.29
  13.8 86.9 %all-gather.5.cloned.1.call-done = bf16[1,512,5376]{2,1,0:T(8,128)(2,1)} async-done(((bf16[1,32,5376]{2,1,0:T(8,128)(2,1)}), bf16[1,512,5376]{2,1,0:T(8,128)(2,1)}) %all-gather.5.cloned.1.call-update) | async-done | bytes 5505040 | tf_op jit(solution)/shard_map/all_gather | solution.py:121
  100.6 4.5 fusion.55
  105.2 3.5 fusion.15
  109.0 2.0 fusion.19
  111.2 0.6 fusion.98
  111.8 0.8 pad_maximum_fusion.1
  112.5 2.0 collective-permute-start.1
  114.5 4.0 collective-permute-start
  118.6 1.6 fusion.13
  120.3 0.3 fusion.41
  120.5 0.8 fusion.128
  121.4 1.9 copy.65
  123.3 2.0 copy.64
  125.3 67.7 %all-gather.7.cloned.1.call-done = bf16[1,512,5376]{2,1,0:T(8,128)(2,1)} async-done(((bf16[1,32,5376]{2,1,0:T(8,128)(2,1)}), bf16[1,512,5376]{2,1,0:T(8,128)(2,1)}) %all-gather.7.cloned.1.call-update) | async-done | bytes 5505040 | tf_op jit(solution)/shard_map/all_gather | solution.py:122
  193.0 4.2 fusion.61
  197.3 3.5 fusion.9
  201.4 1.1 maximum_maximum_fusion
  202.5 1.6 fusion.21
  204.1 1.5 fusion.5
  205.6 2.2 fusion.75
  207.8 3.3 fusion.31
  211.1 2.8 fusion.22
  214.0 2.2 convolution_bitcast_fusion.1
  216.2 1.4 convolution_bitcast_fusion
  217.5 0.9 convolution_convert_fusion
  218.5 75.9 %psum.54 = bf16[512,16]{1,0:T(8,128)(2,1)} all-reduce(bf16[512,16]{1,0:T(8,128)(2,1)} %convolution_convert_fusion), channel_id=1, replica_groups=mesh['dp'=2,'context'=8,'tensor'=16] {'tensor'}, use_global_device_ids=true, to_apply=%region_7.8 | all-reduce | flops 8192 | bytes 32768 | tf_op jit(solution)/shard_map/psum | solution.py:269
  294.3 4.2 fusion
  298.6 1.6 add_convert_fusion.1
  300.1 1.2 fusion.34
  301.4 0.8 fusion.127
  302.2 1.3 collective-permute-start.2
  303.5 1.3 collective-permute-start.3
  304.8 0.9 pad_maximum_fusion.3
  305.7 1.8 copy.40
  307.5 1.1 fusion.64
  308.6 6.3 collective-permute-done.3
  314.8 1.2 fusion.74
  316.1 0.8 fusion.66
  317.0 7.3 fusion.35
  324.3 0.6 fusion.91
  325.1 5.6 fusion.38
  330.7 5.7 fusion.99
  336.4 14.6 %add_convert_fusion = bf16[512,5376]{1,0:T(8,128)(2,1)} fusion(f32[512,5376]{1,0:T(8,128)} %fusion.99, f32[512,5376]{1,0:T(8,128)} %fusion.35, f32[512,5376]{1,0:T(8,128)} %fusion.38, bf16[512,256]{0,1:T(8,128)(2,1)S(1)} %bitcast.198, bf16[5376,256]{1,0:T(8,128)(2,1)S(1)} %copy-done), kind=kOutput, calls=%fused_computation | convolution fusion | flops 1420296192 | bytes 41549824 | tf_op jit(solution)/shard_map/th,dh->td/dot_general | solution.py:284
  351.0 1.8 convolution_convert_fusion.1
  352.8 1.5 fusion.67
  354.3 114.1 %all-reduce.10.cloned.1.call-done = bf16[16,5376]{1,0:T(8,128)(2,1)} async-done(((bf16[16,5376]{1,0:T(8,128)(2,1)}), bf16[16,5376]{1,0:T(8,128)(2,1)}) %all-reduce.10.cloned.1.call-update) | async-done | bytes 172048 | tf_op jit(solution)/shard_map/psum | solution.py:280
  468.5 1.7 convert_element_type.152
  470.1 1.0 fusion.71
  471.2 0.9 fusion.70
  472.0 90.5 %all-reduce.1 = (bf16[16,256]{1,0:T(8,128)(2,1)S(1)}, bf16[2,16,128]{2,1,0:T(8,128)(2,1)S(1)}, bf16[16,256]{1,0:T(8,128)(2,1)S(1)}) all-reduce(bf16[16,256]{1,0:T(8,128)(2,1)} %fusion.67, bf16[2,16,128]{2,1,0:T(8,128)(2,1)S(1)} %pad_maximum_fusion.12, ...), channel_id=1, replica_groups=mesh['dp'=2,'context'=8,'tensor'=16] {'dp','context'}, use_global_device_ids=true, to_apply=%region_4.5 | all-reduce | flops 12288 | bytes 49152 | tf_op jit(solution)/shard_map/psum | solution.py:275
  562.6 0.6 convert_element_type.145
  563.2 0.6 convert_element_type.147
  563.8 0.6 convert_element_type.149
  564.4 4.7 fusion.11
  569.1 85.8 %all-reduce.6.cloned.1.call-done = bf16[512,5376]{1,0:T(8,128)(2,1)} async-done(((bf16[512,5376]{1,0:T(8,128)(2,1)}), bf16[512,5376]{1,0:T(8,128)(2,1)}) %all-reduce.6.cloned.1.call-update) | async-done | bytes 5505040 | tf_op jit(solution)/shard_map/psum | solution.py:291
  654.9 1.7 fusion.77
  656.6 261.6 %all-reduce.8.cloned.1.call-done = f32[3,16,5376]{2,1,0:T(8,128)} async-done(((f32[3,16,5376]{2,1,0:T(8,128)}), f32[3,16,5376]{2,1,0:T(8,128)}) %all-reduce.8.cloned.1.call-update) | async-done | bytes 1032208 | tf_op jit(solution)/shard_map/psum | solution.py:273
  918.1 2.2 copy.69
  (90 shorter events, 1.5 us)
Async XLA Ops:
  7.2 111.4 %copy-start = (bf16[5376,256]{1,0:T(8,128)(2,1)S(1)}, bf16[5376,256]{1,0:T(8,128)(2,1)}, u32[]{:S(2)}) copy-start(bf16[5376,256]{1,0:T(8,128)(2,1)} %param.14) | copy-start | bytes 8257540
  7.2 93.5 %all-gather.5.cloned.1.call-start = ((), (), s32[]{:S(2)}) async-start(), calls=%async_computation.3 | async-start | bytes 5849088 | tf_op jit(solution)/shard_map/all_gather | solution.py:121
  7.9 185.1 %all-gather.7.cloned.1.call-start = ((), (), s32[]{:S(2)}) async-start(), calls=%async_computation.4 | async-start | bytes 5849088 | tf_op jit(solution)/shard_map/all_gather | solution.py:122
  8.7 459.8 %all-reduce.10.cloned.1.call-start = ((), (), s32[]{:S(2)}) async-start(), calls=%async_computation.2 | async-start | bytes 344064 | tf_op jit(solution)/shard_map/psum | solution.py:280
  8.7 102.4 %copy-start.32 = (f32[64]{0:T(128)}, f32[64]{0:T(128)S(1)}, u32[]{:S(2)}) copy-start(f32[64]{0:T(128)S(1)} %negate_power_fusion) | copy-start | bytes 772
  8.8 102.4 %copy-start.26 = (f32[512]{0:T(512)}, f32[512]{0:T(512)S(1)}, u32[]{:S(2)}) copy-start(f32[512]{0:T(512)S(1)} %fusion.114) | copy-start | bytes 6148
  100.6 4.5 copy-start.1
  105.2 15.1 %copy-start.20 = (bf16[512,48]{0,1:T(8,128)(2,1)}, bf16[512,48]{0,1:T(8,128)(2,1)S(1)}, u32[]{:S(2)}) copy-start(bf16[512,48]{0,1:T(8,128)(2,1)S(1)} %fusion.55) | copy-start | bytes 147460
  105.2 3.5 copy-start.30
  105.2 3.7 copy-start.3
  108.9 3.6 copy-start.13
  111.2 9.1 copy-start.29
  111.8 2.8 copy-start.16
  111.8 2.8 copy-start.18
  112.5 88.8 %collective-permute-start.1 = (bf16[2,512,1,128]{1,3,2,0:T(8,128)(2,1)}, bf16[2,512,1,128]{1,3,2,0:T(8,128)(2,1)}, u32[]{:S(2)}, u32[]{:S(2)}) collective-permute-start(bf16[2,512,1,128]{1,3,2,0:T(8,128)(2,1)} %pad_maximum_fusion.1), channel_id=1, source_target_pairs={{0,16},{16,32},{32,48},{48,64},{64,80},{80,96},{96,112},{1,17},{17... | collective-permute-start | bytes 786440 | tf_op jit(solution)/shard_map/ppermute | solution.py:16
  114.5 86.8 %collective-permute-start = (bf16[2,512,1,128]{1,3,2,0:T(8,128)(2,1)}, bf16[2,512,1,128]{1,3,2,0:T(8,128)(2,1)}, u32[]{:S(2)}, u32[]{:S(2)}) collective-permute-start(bf16[2,512,1,128]{1,3,2,0:T(8,128)(2,1)} %pad_maximum_fusion.1), channel_id=1, source_target_pairs={{0,32},{16,48},{32,64},{48,80},{64,96},{80,112},{1,33},{17,49},{33... | collective-permute-start | bytes 786440 | tf_op jit(solution)/shard_map/ppermute | solution.py:16
  193.0 4.2 copy-start.2
  197.2 3.9 copy-start.24
  197.2 3.6 copy-start.28
  197.3 3.9 copy-start.8
  197.3 3.9 copy-start.9
  197.3 3.9 copy-start.10
  197.3 3.9 copy-start.11
  197.3 4.0 copy-start.14
  197.3 4.0 copy-start.17
  197.3 4.0 copy-start.19
  207.8 9.7 %copy-start.15 = (bf16[128,2,512]{2,0,1:T(8,128)(2,1)}, bf16[128,2,512]{2,0,1:T(8,128)(2,1)S(1)}, u32[]{:S(2)}) copy-start(bf16[128,2,512]{2,0,1:T(8,128)(2,1)S(1)} %get-tuple-element.26) | copy-start | bytes 786436
  298.5 356.3 %all-reduce.6.cloned.1.call-start = ((), (), s32[]{:S(2)}) async-start(), calls=%async_computation | async-start | bytes 11010048 | tf_op jit(solution)/shard_map/psum | solution.py:291
  302.2 6.4 collective-permute-start.2
  303.5 11.3 %collective-permute-start.3 = (bf16[2,512,1,128]{1,3,2,0:T(8,128)(2,1)}, bf16[2,512,1,128]{1,3,2,0:T(8,128)(2,1)}, u32[]{:S(2)}, u32[]{:S(2)}) collective-permute-start(bf16[2,512,1,128]{1,3,2,0:T(8,128)(2,1)} %get-tuple-element.14), channel_id=1, source_target_pairs={{32,0},{48,16},{64,32},{80,48},{96,64},{112,80},{33,1},{49,17},{65... | collective-permute-start | bytes 786440 | tf_op jit(solution)/shard_map/ppermute | solution.py:16
  316.1 8.2 copy-start.5
  316.9 13.8 %copy-start.23 = (bf16[512,16]{0,1:T(8,128)(2,1)}, bf16[512,16]{0,1:T(8,128)(2,1)S(1)}, u32[]{:S(2)}) copy-start(bf16[512,16]{0,1:T(8,128)(2,1)S(1)} %fusion.66) | copy-start | bytes 49156
  316.9 7.4 copy-start.27
  317.0 7.4 copy-start.33
  317.0 7.9 copy-start.31
  317.0 8.1 copy-start.4
  324.9 5.8 copy-start.21
  324.9 5.8 copy-start.22
  325.0 5.7 copy-start.25
  325.0 5.7 copy-start.12
  330.7 5.7 copy-start.7
  351.0 120.2 %copy-start.6 = (f32[2,512,1,128]{1,3,2,0:T(8,128)S(1)}, f32[2,512,1,128]{1,3,2,0:T(8,128)}, u32[]{:S(2)}) copy-start(f32[2,512,1,128]{1,3,2,0:T(8,128)} %copy-done.5) | copy-start | bytes 1572868
  351.0 567.1 %all-reduce.8.cloned.1.call-start = ((), (), s32[]{:S(2)}) async-start(), calls=%async_computation.1 | async-start | bytes 2064384 | tf_op jit(solution)/shard_map/psum | solution.py:273
Sparse Core Ops, SparseCore 0:
  9.8 90.8 all-gather.4
  102.4 90.5 all-gather.6
  298.6 169.7 all-reduce.9
  471.0 183.8 all-reduce.5
  660.7 257.3 all-reduce.7
where the time goes:
time: 928 us; the launch traced here: 927 us
  waiting for transfers between devices  624 us (67%)
  blocking collectives  166 us (18%)
  matrix products  84.1 us (9%)
  other arithmetic  19 us (2%)
  between operations  14.4 us (2%)
  local copies, waits for them, and re-layouts  10.5 us (1%)
    psum x1, waiting for transfers between devices, local(): grad_down_qkv = lax.psum(grad_down_part, ('dp', 'context', 'tensor'))  262 us
    psum x1, waiting for transfers between devices, local(): lax.psum(output_up_gradient_piece.astype(jnp.bfloat16), ('dp', 'context'))  114 us
    psum x1, blocking collectives, local(): lax.psum(query_up_gradient_piece.astype(jnp.bfloat16), ('dp', 'context'))  90.5 us
    all_gather x1, waiting for transfers between devices, local(): lax.all_gather(tokens[0], 'tensor', axis=0, tiled=True)  86.9 us
    psum x1, waiting for transfers between devices, local(): lax.psum((term + jnp.dot(hidden_all, down_factors_all, preferred_element_...  85.8 us
    psum x1, blocking collectives, local(): factor_value = lax.psum(factor_part.astype(jnp.bfloat16), 'tensor')  75.9 us
    all_gather x1, waiting for transfers between devices, local(): lax.all_gather(output_gradient[0], 'tensor', axis=0, tiled=True)  67.7 us
  transfers between devices with their start and end apart: 9, of which 6 were waited for; matrix products, arithmetic and copies ran while one was open for 10% of the time, Pallas kernels for 0%

commit v1 on v0

--- a/solution.py
+++ b/solution.py
@@ -277,7 +277,7 @@
         ),
         lax.psum(grad_up_kv_part.astype(jnp.bfloat16), ("dp", "context")).astype(jnp.float32),
         lax.psum(grad_down_out_part.astype(jnp.bfloat16), ("dp", "context")).astype(jnp.float32),
-        lax.psum(output_up_gradient_piece.astype(jnp.bfloat16), ("dp", "context")).astype(
+        lax.psum(lax.psum(output_up_gradient_piece.astype(jnp.bfloat16), "dp"), "context").astype(
             jnp.float32
         ),
     )

time: 928 us -> 863 us (0.930)
  waiting for transfers between devices: 624 us -> 557 us
    psum x1 -> x2, waiting for transfers between devices: 114 us -> 53.4 us  [the longest x1 30.9 us: local(): lax.psum(output_up_gradient_piece.astype(jnp.bfloat16), 'dp')]
  transfers between devices with their start and end apart: 9 -> 10, of which waited for: 6 -> 6; matrix products, arithmetic and copies ran while one was open for 10% -> 10% of each run, Pallas kernels for 0% -> 0%
where the time goes in v1:
time: 863 us; the launch traced here: 862 us
  waiting for transfers between devices  557 us (65%)
  blocking collectives  167 us (19%)
  matrix products  84.1 us (10%)
  other arithmetic  19 us (2%)
  between operations  14.8 us (2%)
  local copies, waits for them, and re-layouts  10.5 us (1%)
  starting transfers between devices  8.84 us (1%)
    psum x1, waiting for transfers between devices, local(): grad_down_qkv = lax.psum(grad_down_part, ('dp', 'context', 'tensor'))  261 us
    psum x1, blocking collectives, local(): lax.psum(query_up_gradient_piece.astype(jnp.bfloat16), ('dp', 'context'))  91.5 us
    all_gather x1, waiting for transfers between devices, local(): lax.all_gather(tokens[0], 'tensor', axis=0, tiled=True)  86.9 us
    psum x1, waiting for transfers between devices, local(): lax.psum((term + jnp.dot(hidden_all, down_factors_all, preferred_element_...  86.2 us
    psum x1, blocking collectives, local(): factor_value = lax.psum(factor_part.astype(jnp.bfloat16), 'tensor')  75.9 us
    all_gather x1, waiting for transfers between devices, local(): lax.all_gather(output_gradient[0], 'tensor', axis=0, tiled=True)  67.7 us
    psum x1, waiting for transfers between devices, local(): lax.psum(output_up_gradient_piece.astype(jnp.bfloat16), 'dp')  30.9 us
    psum x1, waiting for transfers between devices, local(): lax.psum(lax.psum(output_up_gradient_piece.astype(jnp.bfloat16), 'dp'), '...  22.5 us
  transfers between devices with their start and end apart: 10, of which 6 were waited for; matrix products, arithmetic and copies ran while one was open for 10% of the time, Pallas kernels for 0%

profile of v1, /device:TPU:2, one launch (start us, length us, event | category | flops | bytes accessed | tf_op | source)
XLA Modules:
  0.0 861.6 jit_solution(3914008466407732296)
XLA Ops:
  7.2 0.7 all-gather.5.cloned.1.call-update
  8.0 0.7 all-gather.7.cloned.1.call-update
  8.8 0.7 constant_dynamic-slice_fusion
  9.5 0.8 pad_dynamic-slice_fusion
  10.3 1.8 multiply_cosine_fusion
  12.1 1.7 fusion.29
  13.8 86.9 %all-gather.5.cloned.1.call-done = bf16[1,512,5376]{2,1,0:T(8,128)(2,1)} async-done(((bf16[1,32,5376]{2,1,0:T(8,128)(2,1)}), bf16[1,512,5376]{2,1,0:T(8,128)(2,1)}) %all-gather.5.cloned.1.call-update) | async-done | bytes 5505040 | tf_op jit(solution)/shard_map/all_gather | solution.py:121
  100.6 4.5 fusion.55
  105.2 3.5 fusion.15
  109.0 2.0 fusion.19
  111.2 0.6 fusion.98
  111.8 0.8 pad_maximum_fusion.1
  112.5 2.0 collective-permute-start.1
  114.5 4.0 collective-permute-start
  118.6 1.6 fusion.13
  120.3 0.3 fusion.41
  120.5 0.8 fusion.128
  121.4 1.9 copy.65
  123.3 2.0 copy.64
  125.3 67.7 %all-gather.7.cloned.1.call-done = bf16[1,512,5376]{2,1,0:T(8,128)(2,1)} async-done(((bf16[1,32,5376]{2,1,0:T(8,128)(2,1)}), bf16[1,512,5376]{2,1,0:T(8,128)(2,1)}) %all-gather.7.cloned.1.call-update) | async-done | bytes 5505040 | tf_op jit(solution)/shard_map/all_gather | solution.py:122
  193.0 4.2 fusion.61
  197.3 3.5 fusion.9
  201.4 1.1 maximum_maximum_fusion
  202.5 1.6 fusion.21
  204.1 1.5 fusion.5
  205.6 2.2 fusion.75
  207.8 3.3 fusion.31
  211.1 2.8 fusion.22
  214.0 2.2 convolution_bitcast_fusion.1
  216.2 1.4 convolution_bitcast_fusion
  217.5 0.9 convolution_convert_fusion
  218.5 75.9 %psum.61 = bf16[512,16]{1,0:T(8,128)(2,1)} all-reduce(bf16[512,16]{1,0:T(8,128)(2,1)} %convolution_convert_fusion), channel_id=1, replica_groups=mesh['dp'=2,'context'=8,'tensor'=16] {'tensor'}, use_global_device_ids=true, to_apply=%region_7.8 | all-reduce | flops 8192 | bytes 32768 | tf_op jit(solution)/shard_map/psum | solution.py:269
  294.3 4.2 fusion
  298.6 1.6 add_convert_fusion.1
  300.1 1.2 fusion.34
  301.4 0.8 fusion.127
  302.2 1.3 collective-permute-start.2
  303.5 1.3 collective-permute-start.3
  304.8 0.9 pad_maximum_fusion.3
  305.7 1.8 copy.40
  307.5 1.1 fusion.64
  308.6 30.9 %all-reduce.11.cloned.1.call-done = bf16[16,5376]{1,0:T(8,128)(2,1)} async-done(((bf16[16,5376]{1,0:T(8,128)(2,1)}), bf16[16,5376]{1,0:T(8,128)(2,1)}) %all-reduce.11.cloned.1.call-update) | async-done | bytes 172048 | tf_op jit(solution)/shard_map/psum | solution.py:280
  339.6 1.2 fusion.74
  340.8 0.8 fusion.66
  341.7 7.3 fusion.35
  349.0 0.6 fusion.91
  349.8 5.6 fusion.38
  355.4 5.7 fusion.99
  361.1 14.6 %add_convert_fusion = bf16[512,5376]{1,0:T(8,128)(2,1)} fusion(f32[512,5376]{1,0:T(8,128)} %fusion.99, f32[512,5376]{1,0:T(8,128)} %fusion.35, f32[512,5376]{1,0:T(8,128)} %fusion.38, bf16[512,256]{0,1:T(8,128)(2,1)S(1)} %bitcast.198, bf16[5376,256]{1,0:T(8,128)(2,1)S(1)} %copy-done), kind=kOutput, calls=%fused_computation | convolution fusion | flops 1420296192 | bytes 41549824 | tf_op jit(solution)/shard_map/th,dh->td/dot_general | solution.py:284
  375.8 1.8 convolution_convert_fusion.1
  377.6 1.5 fusion.67
  379.1 22.5 %all-reduce.13.cloned.1.call-done = bf16[16,5376]{1,0:T(8,128)(2,1)} async-done(((bf16[16,5376]{1,0:T(8,128)(2,1)}), bf16[16,5376]{1,0:T(8,128)(2,1)}) %all-reduce.13.cloned.1.call-update) | async-done | bytes 172048 | tf_op jit(solution)/shard_map/psum | solution.py:280
  401.6 1.7 convert_element_type.152
  403.2 1.0 fusion.71
  404.3 0.9 fusion.70
  405.1 91.5 %all-reduce.1 = (bf16[16,256]{1,0:T(8,128)(2,1)S(1)}, bf16[2,16,128]{2,1,0:T(8,128)(2,1)S(1)}, bf16[16,256]{1,0:T(8,128)(2,1)S(1)}) all-reduce(bf16[16,256]{1,0:T(8,128)(2,1)} %fusion.67, bf16[2,16,128]{2,1,0:T(8,128)(2,1)S(1)} %pad_maximum_fusion.12, ...), channel_id=1, replica_groups=mesh['dp'=2,'context'=8,'tensor'=16] {'dp','context'}, use_global_device_ids=true, to_apply=%region_4.5 | all-reduce | flops 12288 | bytes 49152 | tf_op jit(solution)/shard_map/psum | solution.py:275
  496.6 0.6 convert_element_type.145
  497.2 0.6 convert_element_type.147
  497.8 0.6 convert_element_type.149
  498.4 4.7 fusion.11
  503.1 86.2 %all-reduce.7.cloned.1.call-done = bf16[512,5376]{1,0:T(8,128)(2,1)} async-done(((bf16[512,5376]{1,0:T(8,128)(2,1)}), bf16[512,5376]{1,0:T(8,128)(2,1)}) %all-reduce.7.cloned.1.call-update) | async-done | bytes 5505040 | tf_op jit(solution)/shard_map/psum | solution.py:291
  589.3 1.7 fusion.77
  591.0 261.4 %all-reduce.9.cloned.1.call-done = f32[3,16,5376]{2,1,0:T(8,128)} async-done(((f32[3,16,5376]{2,1,0:T(8,128)}), f32[3,16,5376]{2,1,0:T(8,128)}) %all-reduce.9.cloned.1.call-update) | async-done | bytes 1032208 | tf_op jit(solution)/shard_map/psum | solution.py:273
  852.5 2.2 copy.70
  (93 shorter events, 1.5 us)
Async XLA Ops:
  7.2 111.4 %copy-start = (bf16[5376,256]{1,0:T(8,128)(2,1)S(1)}, bf16[5376,256]{1,0:T(8,128)(2,1)}, u32[]{:S(2)}) copy-start(bf16[5376,256]{1,0:T(8,128)(2,1)} %param.14) | copy-start | bytes 8257540
  7.2 93.5 %all-gather.5.cloned.1.call-start = ((), (), s32[]{:S(2)}) async-start(), calls=%async_computation.4 | async-start | bytes 5849088 | tf_op jit(solution)/shard_map/all_gather | solution.py:121
  7.9 185.1 %all-gather.7.cloned.1.call-start = ((), (), s32[]{:S(2)}) async-start(), calls=%async_computation.5 | async-start | bytes 5849088 | tf_op jit(solution)/shard_map/all_gather | solution.py:122
  8.7 330.8 %all-reduce.11.cloned.1.call-start = ((), (), s32[]{:S(2)}) async-start(), calls=%async_computation.2 | async-start | bytes 344064 | tf_op jit(solution)/shard_map/psum | solution.py:280
  8.7 102.4 %copy-start.32 = (f32[64]{0:T(128)}, f32[64]{0:T(128)S(1)}, u32[]{:S(2)}) copy-start(f32[64]{0:T(128)S(1)} %negate_power_fusion) | copy-start | bytes 772
  8.8 102.4 %copy-start.26 = (f32[512]{0:T(512)}, f32[512]{0:T(512)S(1)}, u32[]{:S(2)}) copy-start(f32[512]{0:T(512)S(1)} %fusion.114) | copy-start | bytes 6148
  100.6 4.5 copy-start.1
  105.2 15.1 %copy-start.20 = (bf16[512,48]{0,1:T(8,128)(2,1)}, bf16[512,48]{0,1:T(8,128)(2,1)S(1)}, u32[]{:S(2)}) copy-start(bf16[512,48]{0,1:T(8,128)(2,1)S(1)} %fusion.55) | copy-start | bytes 147460
  105.2 3.5 copy-start.30
  105.2 3.7 copy-start.3
  108.9 3.6 copy-start.13
  111.2 9.1 %copy-start.29 = (bf16[16,256]{1,0:T(8,128)(2,1)S(1)}, bf16[16,256]{1,0:T(8,128)(2,1)}, u32[]{:S(2)}) copy-start(bf16[16,256]{1,0:T(8,128)(2,1)} %param.18) | copy-start | bytes 24580
  111.8 2.8 copy-start.16
  111.8 2.8 copy-start.18
  112.5 88.8 %collective-permute-start.1 = (bf16[2,512,1,128]{1,3,2,0:T(8,128)(2,1)}, bf16[2,512,1,128]{1,3,2,0:T(8,128)(2,1)}, u32[]{:S(2)}, u32[]{:S(2)}) collective-permute-start(bf16[2,512,1,128]{1,3,2,0:T(8,128)(2,1)} %pad_maximum_fusion.1), channel_id=1, source_target_pairs={{0,16},{16,32},{32,48},{48,64},{64,80},{80,96},{96,112},{1,17},{17... | collective-permute-start | bytes 786440 | tf_op jit(solution)/shard_map/ppermute | solution.py:16
  114.5 86.8 %collective-permute-start = (bf16[2,512,1,128]{1,3,2,0:T(8,128)(2,1)}, bf16[2,512,1,128]{1,3,2,0:T(8,128)(2,1)}, u32[]{:S(2)}, u32[]{:S(2)}) collective-permute-start(bf16[2,512,1,128]{1,3,2,0:T(8,128)(2,1)} %pad_maximum_fusion.1), channel_id=1, source_target_pairs={{0,32},{16,48},{32,64},{48,80},{64,96},{80,112},{1,33},{17,49},{33... | collective-permute-start | bytes 786440 | tf_op jit(solution)/shard_map/ppermute | solution.py:16
  193.0 4.2 copy-start.2
  197.2 3.9 copy-start.24
  197.2 3.6 copy-start.28
  197.3 3.9 copy-start.8
  197.3 3.9 copy-start.9
  197.3 3.9 copy-start.10
  197.3 3.9 copy-start.11
  197.3 4.0 copy-start.14
  197.3 4.0 copy-start.17
  197.3 4.0 copy-start.19
  207.8 9.7 %copy-start.15 = (bf16[128,2,512]{2,0,1:T(8,128)(2,1)}, bf16[128,2,512]{2,0,1:T(8,128)(2,1)S(1)}, u32[]{:S(2)}) copy-start(bf16[128,2,512]{2,0,1:T(8,128)(2,1)S(1)} %get-tuple-element.26) | copy-start | bytes 786436
  298.5 103.0 %all-reduce.13.cloned.1.call-start = ((), (), s32[]{:S(2)}) async-start(), calls=%async_computation.3 | async-start | bytes 344064 | tf_op jit(solution)/shard_map/psum | solution.py:280
  302.2 37.3 %collective-permute-start.2 = (bf16[2,512,1,128]{1,3,2,0:T(8,128)(2,1)}, bf16[2,512,1,128]{1,3,2,0:T(8,128)(2,1)}, u32[]{:S(2)}, u32[]{:S(2)}) collective-permute-start(bf16[2,512,1,128]{1,3,2,0:T(8,128)(2,1)} %get-tuple-element.13), channel_id=1, source_target_pairs={{16,0},{32,16},{48,32},{64,48},{80,64},{96,80},{112,96},{17,1},{33... | collective-permute-start | bytes 786440 | tf_op jit(solution)/shard_map/ppermute | solution.py:16
  303.5 36.1 %collective-permute-start.3 = (bf16[2,512,1,128]{1,3,2,0:T(8,128)(2,1)}, bf16[2,512,1,128]{1,3,2,0:T(8,128)(2,1)}, u32[]{:S(2)}, u32[]{:S(2)}) collective-permute-start(bf16[2,512,1,128]{1,3,2,0:T(8,128)(2,1)} %get-tuple-element.14), channel_id=1, source_target_pairs={{32,0},{48,16},{64,32},{80,48},{96,64},{112,80},{33,1},{49,17},{65... | collective-permute-start | bytes 786440 | tf_op jit(solution)/shard_map/ppermute | solution.py:16
  339.5 249.8 %all-reduce.7.cloned.1.call-start = ((), (), s32[]{:S(2)}) async-start(), calls=%async_computation | async-start | bytes 11010048 | tf_op jit(solution)/shard_map/psum | solution.py:291
  340.8 8.2 copy-start.5
  341.7 13.8 %copy-start.23 = (bf16[512,16]{0,1:T(8,128)(2,1)}, bf16[512,16]{0,1:T(8,128)(2,1)S(1)}, u32[]{:S(2)}) copy-start(bf16[512,16]{0,1:T(8,128)(2,1)S(1)} %fusion.66) | copy-start | bytes 49156
  341.7 7.4 copy-start.27
  341.7 7.3 copy-start.33
  341.7 7.9 copy-start.31
  341.7 8.1 copy-start.4
  349.6 5.8 copy-start.21
  349.6 5.8 copy-start.22
  349.8 5.7 copy-start.25
  349.8 5.7 copy-start.12
  355.4 5.7 copy-start.7
  375.7 28.6 %copy-start.6 = (f32[2,512,1,128]{1,3,2,0:T(8,128)S(1)}, f32[2,512,1,128]{1,3,2,0:T(8,128)}, u32[]{:S(2)}) copy-start(f32[2,512,1,128]{1,3,2,0:T(8,128)} %copy-done.5) | copy-start | bytes 1572868
  375.7 476.8 %all-reduce.9.cloned.1.call-start = ((), (), s32[]{:S(2)}) async-start(), calls=%async_computation.1 | async-start | bytes 2064384 | tf_op jit(solution)/shard_map/psum | solution.py:273
Sparse Core Ops, SparseCore 0:
  9.8 90.8 all-gather.4
  102.4 90.5 all-gather.6
  298.6 40.7 all-reduce.10
  341.7 59.8 all-reduce.12
  404.1 185.1 all-reduce.6
  595.2 257.2 all-reduce.8
